TPU v7x, 32 devices: a whole 2x2x4 slice. The times are simulated.
32 devices in a mesh: row: 8 (over z, y), col: 4 (over x, core).
Axes of the slice: x: 2, y: 2, z: 4, core: 2. Of those that a mesh axis runs over, the one named last changes fastest.
Arguments:
- activations: bfloat16 [512, 28672], P('col', 'row'), may hold values from -36 to 36
- output_gradient: bfloat16 [512, 8192], P('row', 'col'), may hold values from -6 to 6
- frozen_weight: bfloat16 [28672, 8192], P('row', 'col'), may hold values from -0.0390625 to 0.0390625
- sparsity_mask_pattern: int32 [7168, 8192], P('row', 'col'), may hold values from 0 to 5
- adapter_left_factor: bfloat16 [28672, 16], P('row'), may hold values from -0.19921875 to 0.19921875
- adapter_right_factor: bfloat16 [16, 8192], P(None, 'col'), may hold values from -0.359375 to 0.359375
Outputs:
- input_grad: bfloat16 [512, 28672], P('col', 'row')
- left_grad: float32 [28672, 16], P('row')
- right_grad: float32 [16, 8192], P(None, 'col')
Inputs may be any that keep to these rules, and one draw needn't show every extreme that they name: `sparsity_mask_pattern`: a pattern number of the 2:4 mask.
All inputs are finite; a program needn't handle non-finite values.
Results may differ from a plain program's by a relative error of at most 0.005.
Values may be sent and summed in bfloat16 or wider, within the bound.
No kernel may reach another device: no remote copies, remote signals or barrier semaphores. Data moves between devices by JAX's collectives and lax.ppermute only.
A program may use at most 192 MiB of HBM per device.

v0:
```python
import jax
import jax.numpy as jnp
from jax import lax
from jax.sharding import PartitionSpec as P

PAIRS = ((0, 1), (0, 2), (0, 3), (1, 2), (1, 3), (2, 3))
ADAPTER_SCALE = 2.0


def expand_mask(code):
    groups = []
    for column in range(4):
        kept = jnp.zeros(code.shape, jnp.float32)
        for pattern in range(6):
            if column in PAIRS[pattern]:
                kept = kept + (code == pattern).astype(jnp.float32)
        groups.append(kept)
    stacked = jnp.stack(groups, axis=1)
    return stacked.reshape(code.shape[0] * 4, code.shape[1])


def input_sums_of(grad_rows, merged):
    return lax.psum_scatter(
        lax.dot_general(
            grad_rows, merged, (((1,), (1,)), ((), ())), preferred_element_type=jnp.float32
        ),
        "col",
        scatter_dimension=0,
        tiled=True,
    )


def weight_grad_of(activations, grad_rows):
    return lax.dot_general(
        lax.all_gather(activations, "col", axis=0, tiled=True),
        grad_rows,
        (((0,), (0,)), ((), ())),
        preferred_element_type=jnp.float32,
    )


def per_device(
    activations,
    output_gradient,
    frozen_weight,
    sparsity_mask_pattern,
    adapter_left_factor,
    adapter_right_factor,
):
    masked = expand_mask(sparsity_mask_pattern)
    low_rank_update = jnp.dot(
        adapter_left_factor, adapter_right_factor, preferred_element_type=jnp.float32
    )
    merged = (
        masked * (frozen_weight.astype(jnp.float32) + ADAPTER_SCALE * low_rank_update)
    ).astype(jnp.bfloat16)
    grad_rows = lax.all_gather(output_gradient, "row", axis=0, tiled=True)
    all_tokens = grad_rows.shape[0]
    first_grad = weight_grad_of(activations, grad_rows)
    weight_grad, later_grads = lax.optimization_barrier((first_grad, grad_rows))
    input_grad = input_sums_of(later_grads, merged).astype(jnp.bfloat16)
    pruned_gradient = (masked * weight_grad / all_tokens).astype(jnp.bfloat16)
    left_partial = ADAPTER_SCALE * lax.dot_general(
        pruned_gradient,
        adapter_right_factor,
        (((1,), (1,)), ((), ())),
        preferred_element_type=jnp.float32,
    )
    right_partial = ADAPTER_SCALE * lax.dot_general(
        adapter_left_factor,
        pruned_gradient,
        (((0,), (0,)), ((), ())),
        preferred_element_type=jnp.float32,
    )
    right_grad = lax.psum(right_partial, "row")
    left_grad = lax.psum(left_partial, "col")
    return (input_grad, left_grad, right_grad)


def solution(mesh):
    in_specs = (
        P("col", "row"),
        P("row", "col"),
        P("row", "col"),
        P("row", "col"),
        P("row", None),
        P(None, "col"),
    )
    out_specs = (P("col", "row"), P("row", None), P(None, "col"))
    return jax.shard_map(
        per_device, mesh=mesh, in_specs=in_specs, out_specs=out_specs, check_vma=False
    )
```

profile of v0, /device:TPU:0, one launch (start us, length us, event | category | flops | bytes accessed | tf_op | source)
XLA Modules:
  0.0 334.8 jit_solution(17214782488458227821)
XLA Ops:
  7.2 0.7 all-gather.5.cloned.1.call-update
  7.9 0.0 all-gather.3.cloned.1.call-start
  8.0 0.7 all-gather.3.cloned.1.call-update
  8.7 0.0 reduce-scatter.2.cloned.1.call-start
  8.7 7.8 %fusion = (f32[896,1,2048]{2,0,1:T(8,128)S(1)}, pred[896,2048]{1,0:T(8,128)(4,1)S(1)}, pred[896,2048]{1,0:T(8,128)(4,1)S(1)}, pred[896,2048]{1,0:T(8,128)(4,1)}) fusion(s32[896,2048]{1,0:T(8,128)} %param.9), kind=kLoop, calls=%fused_computation.11 | loop fusion | flops 14680064 | bytes 20185088 | tf_op jit(solution)/shard_map/stack | solution.py:18
  16.6 6.5 %fusion.1 = (f32[896,1,2048]{2,0,1:T(8,128)S(1)}, pred[896,2048]{1,0:T(8,128)(4,1)S(1)}, pred[896,2048]{1,0:T(8,128)(4,1)}) fusion(pred[896,2048]{1,0:T(8,128)(4,1)S(1)} %get-tuple-element.8, s32[896,2048]{1,0:T(8,128)} %param.9), kind=kLoop, calls=%fused_computation.12 | loop fusion | flops 12845056 | bytes 20185088 | tf_op jit(solution)/shard_map/stack | solution.py:18
  23.1 3.6 %fusion.2 = (f32[896,1,2048]{2,0,1:T(8,128)S(1)}, pred[896,2048]{1,0:T(8,128)(4,1)}) fusion(pred[896,2048]{1,0:T(8,128)(4,1)S(1)} %get-tuple-element.12, pred[896,2048]{1,0:T(8,128)(4,1)S(1)} %get-tuple-element.9, s32[896,2048]{1,0:T(8,128)S(1)} %bitcast.20), kind=kLoop, calls=%fused_computation.13 | loop fusion | flops 11010048 | bytes 20185088 | tf_op jit(solution)/shard_map/stack | solution.py:18
  26.7 5.1 %fusion.3 = f32[896,1,2048]{2,0,1:T(8,128)S(1)} fusion(pred[896,2048]{1,0:T(8,128)(4,1)} %get-tuple-element.15, pred[896,2048]{1,0:T(8,128)(4,1)} %get-tuple-element.13, pred[896,2048]{1,0:T(8,128)(4,1)} %get-tuple-element.10), kind=kLoop, calls=%fused_computation.14 | loop fusion | flops 9175040 | bytes 12845056 | tf_op jit(solution)/shard_map/stack | solution.py:18
  31.8 10.3 %pad_maximum_fusion = f32[896,4,2048]{2,0,1:T(8,128)} fusion(f32[896,1,2048]{2,0,1:T(8,128)S(1)} %fusion.3, f32[896,1,2048]{2,0,1:T(8,128)S(1)} %get-tuple-element.14, f32[896,1,2048]{2,0,1:T(8,128)S(1)} %get-tuple-element.11, f32[896,1,2048]{2,0,1:T(8,128)S(1)} %get-tuple-element.7), kind=kLoop, calls=%fused_computation | loop fusion | flops 22020096 | bytes 58720256 | tf_op jit(solution)/shard_map/stack | solution.py:18
  42.1 33.6 %copy.9 = f32[896,4,2048]{2,1,0:T(4,128)} copy(f32[896,4,2048]{2,0,1:T(8,128)} %pad_maximum_fusion) | data formatting | bytes 58720256 | tf_op jit(solution)/shard_map/stack | solution.py:18
  75.7 33.5 %reshape.9 = f32[3584,2048]{1,0:T(8,128)} reshape(f32[896,4,2048]{2,1,0:T(4,128)} %copy.9) | data formatting | bytes 58720256 | tf_op jit(solution)/shard_map/reshape | solution.py:19
  109.2 16.2 %fusion.7 = f32[3584,2048]{1,0:T(8,128)} fusion(bf16[512,3584]{1,0:T(8,128)(2,1)} %all-gather.3.cloned.1.call-done, bf16[512,2048]{1,0:T(8,128)(2,1)} %all-gather.5.cloned.1.call-done), kind=kOutput, calls=%fused_computation.26 | convolution fusion | flops 7516192768 | bytes 35127296 | tf_op jit(solution)/shard_map/dot_general | solution.py:34
  125.4 21.5 %fusion.4 = f32[512,3584]{1,0:T(8,128)} fusion(bf16[512,2048]{1,0:T(8,128)(2,1)S(1)} %copy-done.2, f32[3584,2048]{1,0:T(8,128)} %reshape.9, bf16[3584,2048]{1,0:T(8,128)(2,1)} %param.8, bf16[3584,16]{0,1:T(8,128)(2,1)S(1)} %copy-done, bf16[16,2048]{1,0:T(8,128)(2,1)S(1)} %copy-done.1), kind=kOutput, calls=%fused_computation.22 | convolution fusion | flops 7787773952 | bytes 53657600 | tf_op jit(solution)/shard_map/dot_general | solution.py:24
  147.0 0.0 all-reduce.3.cloned.1.call-start
  147.0 26.9 %multiply_convert_fusion = bf16[3584,2048]{1,0:T(8,128)(2,1)} fusion(f32[3584,2048]{1,0:T(8,128)} %reshape.9, f32[3584,2048]{1,0:T(8,128)} %fusion.7), kind=kLoop, calls=%fused_computation.1 | loop fusion | flops 22020096 | bytes 73400320 | tf_op jit(solution)/shard_map/convert_element_type | solution.py:62
  173.9 9.9 %convolution_multiply_fusion = f32[3584,16]{0,1:T(8,128)} fusion(bf16[3584,2048]{1,0:T(8,128)(2,1)} %multiply_convert_fusion, bf16[16,2048]{1,0:T(8,128)(2,1)S(1)} %copy-done.1), kind=kOutput, calls=%fused_computation.15 | convolution fusion | flops 234938368 | bytes 14974976 | tf_op jit(solution)/shard_map/dot_general | solution.py:63
  183.8 0.0 all-reduce.5.cloned.1.call-start
  183.9 8.0 %fusion.5 = f32[16,2048]{1,0:T(8,128)} fusion(bf16[3584,16]{0,1:T(8,128)(2,1)S(1)} %copy-done, bf16[3584,2048]{1,0:T(8,128)(2,1)} %multiply_convert_fusion), kind=kOutput, calls=%fused_computation.24 | convolution fusion | flops 234913792 | bytes 14925824 | tf_op jit(solution)/shard_map/dot_general | solution.py:69
  191.9 24.0 %reduce-scatter.2.cloned.1.call-done = f32[128,3584]{1,0:T(8,128)} async-done(((f32[512,3584]{1,0:T(8,128)}), f32[128,3584]{1,0:T(8,128)}) %reduce-scatter.2.cloned.1.call-update) | async-done | bytes 1835024 | tf_op jit(solution)/shard_map/reduce_scatter | solution.py:23
  215.9 2.5 convert_element_type.44
  218.4 32.5 %all-reduce.3.cloned.1.call-done = f32[3584,16]{0,1:T(8,128)} async-done(((f32[3584,16]{0,1:T(8,128)}), f32[3584,16]{0,1:T(8,128)}) %all-reduce.3.cloned.1.call-update) | async-done | bytes 229392 | tf_op jit(solution)/shard_map/psum | solution.py:76
  250.9 74.2 %all-reduce.5.cloned.1.call-done = f32[16,2048]{1,0:T(8,128)} async-done(((f32[16,2048]{1,0:T(8,128)}), f32[16,2048]{1,0:T(8,128)}) %all-reduce.5.cloned.1.call-update) | async-done | bytes 131088 | tf_op jit(solution)/shard_map/psum | solution.py:75
  325.0 1.6 copy.12
  326.7 1.6 copy.13
  (17 shorter events, 0.1 us)
Async XLA Ops:
  7.2 118.2 %copy-start = (bf16[3584,16]{0,1:T(8,128)(2,1)S(1)}, bf16[3584,16]{0,1:T(8,128)(2,1)}, u32[]{:S(2)}) copy-start(bf16[3584,16]{0,1:T(8,128)(2,1)} %param.10) | copy-start | bytes 344068
  7.2 102.0 %all-gather.5.cloned.1.call-start = ((), (), s32[]{:S(2)}) async-start(), calls=%async_computation.2 | async-start | bytes 2359296 | tf_op jit(solution)/shard_map/all_gather | solution.py:57
  7.9 101.3 %all-gather.3.cloned.1.call-start = ((), (), s32[]{:S(2)}) async-start(), calls=%async_computation.1 | async-start | bytes 4587520 | tf_op jit(solution)/shard_map/all_gather | solution.py:35
  8.7 207.2 %reduce-scatter.2.cloned.1.call-start = ((), (), s32[]{:S(2)}) async-start(), calls=%async_computation.3 | async-start | bytes 9175040 | tf_op jit(solution)/shard_map/reduce_scatter | solution.py:23
  8.7 14.4 %slice-start = ((s8[7340032]{0:T(1024)(128)(4,1)}), s8[4194304]{0:T(1024)(128)(4,1)S(1)}, s32[]{:S(2)}) async-start(s8[7340032]{0:T(1024)(128)(4,1)} %bitcast.19), calls=%async_computation.6 | async-start | bytes 8388608
  16.5 6.5 %slice-start.1 = ((s8[7340032]{0:T(1024)(128)(4,1)}), s8[3145728]{0:T(1024)(128)(4,1)S(1)}, s32[]{:S(2)}) async-start(s8[7340032]{0:T(1024)(128)(4,1)} %bitcast.19), calls=%async_computation.7 | async-start | bytes 6291456
  109.2 16.2 %copy-start.1 = (bf16[16,2048]{1,0:T(8,128)(2,1)S(1)}, bf16[16,2048]{1,0:T(8,128)(2,1)}, u32[]{:S(2)}) copy-start(bf16[16,2048]{1,0:T(8,128)(2,1)} %param.11) | copy-start | bytes 196612
  109.2 16.2 %copy-start.2 = (bf16[512,2048]{1,0:T(8,128)(2,1)S(1)}, bf16[512,2048]{1,0:T(8,128)(2,1)}, u32[]{:S(2)}) copy-start(bf16[512,2048]{1,0:T(8,128)(2,1)} %all-gather.5.cloned.1.call-done) | copy-start | bytes 6291460
  147.0 103.9 %all-reduce.3.cloned.1.call-start = ((), (), s32[]{:S(2)}) async-start(), calls=%async_computation.4 | async-start | bytes 458752 | tf_op jit(solution)/shard_map/psum | solution.py:76
  183.8 141.2 %all-reduce.5.cloned.1.call-start = ((), (), s32[]{:S(2)}) async-start(), calls=%async_computation.5 | async-start | bytes 262144 | tf_op jit(solution)/shard_map/psum | solution.py:75
Sparse Core Ops, SparseCore 0:
  10.1 51.8 all-gather.4
  63.5 29.9 all-gather.2
  147.1 68.7 reduce-scatter.1
  218.6 32.1 all-reduce.2
  254.6 70.3 all-reduce.4
where the time goes:
time: 336 us; the launch traced here: 335 us
  waiting for transfers between devices  132 us (39%)
  local copies, waits for them, and re-layouts  70.4 us (21%)
  other arithmetic  62.8 us (19%)
  matrix products  55.6 us (17%)
  between operations  13.8 us (4%)
    psum x1, waiting for transfers between devices, per_device(): right_grad = lax.psum(right_partial, 'row')  74.2 us
    another operation x1, local copies, waits for them, and re-layouts, expand_mask(): stacked = jnp.stack(groups, axis=1)  33.6 us
    reshape x1, local copies, waits for them, and re-layouts, expand_mask(): return stacked.reshape(code.shape[0] * 4, code.shape[1])  33.5 us
    another operation x5, other arithmetic, expand_mask(): stacked = jnp.stack(groups, axis=1)  33.3 us
    psum x1, waiting for transfers between devices, per_device(): left_grad = lax.psum(left_partial, 'col')  32.5 us
    convert_element_type x1, other arithmetic, per_device(): pruned_gradient = (masked * weight_grad / all_tokens).astype(jnp.bfloat16)  26.9 us
    reduce_scatter x1, waiting for transfers between devices, input_sums_of(): lax.psum_scatter(lax.dot_general(grad_rows, merged, (((1,), (1,)), ((), (...  24 us
    dot_general x1, matrix products, input_sums_of(): lax.dot_general(grad_rows, merged, (((1,), (1,)), ((), ())), preferred_el...  21.5 us
  transfers between devices with their start and end apart: 5, of which 3 were waited for; matrix products, arithmetic and copies ran while one was open for 44% of the time, Pallas kernels for 0%

commit v1 on v0

v1 whole, which is shorter than its diff:
```python
import functools

import jax
import jax.numpy as jnp
from jax import lax
from jax.experimental import pallas as pl
from jax.experimental.pallas import tpu as pltpu
from jax.sharding import PartitionSpec as P

PAIRS = ((0, 1), (0, 2), (0, 3), (1, 2), (1, 3), (2, 3))
KEPT = tuple(sum(1 << p for p, pair in enumerate(PAIRS) if j in pair) for j in range(4))
ADAPTER_SCALE = 2.0
LANES = 128
F32, BF16 = jnp.float32, jnp.bfloat16
VMEM_BYTES = 56 * 1024 * 1024


def tile_of(extent, most):
    tile = most
    while extent % tile:
        tile -= LANES
    return tile


def params():
    return pltpu.CompilerParams(vmem_limit_bytes=VMEM_BYTES)


def cost(flops, nbytes):
    return pl.CostEstimate(flops=flops, bytes_accessed=nbytes, transcendentals=0)


def merge_kernel(code_ref, w_ref, lt_ref, r_ref, merged_ref, mask_ref, expand):
    groups, cols = code_ref.shape
    rows = 4 * groups
    for c in range(cols // LANES):
        code = code_ref[:, pl.ds(c * LANES, LANES)]
        for j in range(4):
            kept = lax.shift_right_logical(jnp.full(code.shape, KEPT[j], jnp.int32), code) & 1
            expand[pl.ds(c * rows + j, groups, stride=4), :] = kept.astype(F32)
    update = lax.dot_general(
        lt_ref[...] * ADAPTER_SCALE, r_ref[...], (((0,), (0,)), ((), ())), preferred_element_type=F32
    )
    for c in range(cols // LANES):
        at = pl.ds(c * LANES, LANES)
        mask = expand[pl.ds(c * rows, rows), :]
        whole = w_ref[:, at].astype(F32) + update[:, c * LANES : (c + 1) * LANES]
        merged_ref[:, at] = (mask * whole).astype(BF16)
        mask_ref[:, at] = mask.astype(BF16)


def merge(code, w, lt, r):
    hid, cols = w.shape
    rank = r.shape[0]
    th = tile_of(hid, 512)
    return pl.pallas_call(
        merge_kernel,
        grid=(hid // th,),
        in_specs=[
            pl.BlockSpec((th // 4, cols), lambda i: (i, 0)),
            pl.BlockSpec((th, cols), lambda i: (i, 0)),
            pl.BlockSpec((rank, th), lambda i: (0, i)),
            pl.BlockSpec((rank, cols), lambda i: (0, 0)),
        ],
        out_specs=[pl.BlockSpec((th, cols), lambda i: (i, 0))] * 2,
        out_shape=[jax.ShapeDtypeStruct((hid, cols), BF16)] * 2,
        scratch_shapes=[pltpu.VMEM((th * cols // LANES, LANES), F32)],
        compiler_params=params(),
        cost_estimate=cost(2 * hid * cols * rank, 9 * hid * cols),
        name="merge",
    )(code, w, lt, r)


def join_kernel(at_ref, *refs):
    *blocks, out_ref = refs
    tall = blocks[0].shape[0]
    for k, block in enumerate(blocks):
        out_ref[pl.ds(pl.multiple_of(at_ref[k], tall), tall), :] = block[...]


def join(at, blocks):
    tall, cols = blocks[0].shape
    n = len(blocks)
    tc = tile_of(cols, 512)
    return pl.pallas_call(
        join_kernel,
        grid_spec=pltpu.PrefetchScalarGridSpec(
            num_scalar_prefetch=1,
            grid=(cols // tc,),
            in_specs=[pl.BlockSpec((tall, tc), lambda i, at: (0, i))] * n,
            out_specs=pl.BlockSpec((n * tall, tc), lambda i, at: (0, i)),
        ),
        out_shape=jax.ShapeDtypeStruct((n * tall, cols), BF16),
        compiler_params=params(),
        cost_estimate=cost(0, 4 * n * tall * cols),
        name="join",
    )(at, *blocks)


def back_kernel(dy_ref, m_ref, keep_ref, send_ref, *, tall):
    p = lax.dot_general(dy_ref[...], m_ref[...], (((1,), (1,)), ((), ())), preferred_element_type=F32)
    for k in range(p.shape[0] // tall):
        out_ref = send_ref if k % 2 else keep_ref
        out_ref[pl.ds(k // 2 * tall, tall), :] = p[k * tall : (k + 1) * tall].astype(out_ref.dtype)


def back(dy, merged, first, count, tall):
    tokens, cols = dy.shape
    th = tile_of(count, 512)
    return pl.pallas_call(
        functools.partial(back_kernel, tall=tall),
        grid=(count // th,),
        in_specs=[
            pl.BlockSpec((tokens, cols), lambda i: (0, 0)),
            pl.BlockSpec((th, cols), lambda i: (i + first // th, 0)),
        ],
        out_specs=[pl.BlockSpec((tokens // 2, th), lambda i: (0, i))] * 2,
        out_shape=[
            jax.ShapeDtypeStruct((tokens // 2, count), F32),
            jax.ShapeDtypeStruct((tokens // 2, count), BF16),
        ],
        compiler_params=params(),
        cost_estimate=cost(2 * tokens * cols * count, 2 * cols * count),
        name="back",
    )(dy, merged)


def adapter_kernel(*refs, parts, scale):
    acts = refs[:parts]
    dy_ref, mask_ref, lt_ref, r_ref, left_in, left_ref, right_ref = refs[parts:]
    act = jnp.concatenate([a[...] for a in acts], axis=0)
    g = lax.dot_general(act, dy_ref[...], (((0,), (0,)), ((), ())), preferred_element_type=F32)
    g = (g * scale).astype(BF16) * mask_ref[...]
    left_ref[...] = left_in[...] + lax.dot_general(
        r_ref[...] * ADAPTER_SCALE, g, (((1,), (1,)), ((), ())), preferred_element_type=F32
    )
    right = lax.dot_general(
        lt_ref[...] * ADAPTER_SCALE, g, (((1,), (0,)), ((), ())), preferred_element_type=F32
    )

    @pl.when(pl.program_id(0) == 0)
    def _():
        right_ref[...] = right

    @pl.when(pl.program_id(0) != 0)
    def _():
        right_ref[...] += right


def adapter(acts, dy, mask, lt, r, left, first, count):
    rank, hid = lt.shape
    tall = acts[0].shape[0]
    tokens = dy.shape[0]
    th = tile_of(hid, 512)
    c = first // count
    return pl.pallas_call(
        functools.partial(adapter_kernel, parts=len(acts), scale=1.0 / tokens),
        grid=(hid // th,),
        in_specs=[pl.BlockSpec((tall, th), lambda i: (0, i))] * len(acts)
        + [
            pl.BlockSpec((tokens, count), lambda i: (0, c)),
            pl.BlockSpec((th, count), lambda i: (i, c)),
            pl.BlockSpec((rank, th), lambda i: (0, i)),
            pl.BlockSpec((rank, count), lambda i: (0, c)),
            pl.BlockSpec((rank, th), lambda i: (0, i)),
        ],
        out_specs=[
            pl.BlockSpec((rank, th), lambda i: (0, i)),
            pl.BlockSpec((rank, count), lambda i: (0, 0)),
        ],
        out_shape=[
            jax.ShapeDtypeStruct((rank, hid), F32),
            jax.ShapeDtypeStruct((rank, count), F32),
        ],
        compiler_params=params(),
        cost_estimate=cost(2 * hid * count * (tokens + 4 * rank), 2 * hid * count),
        name="adapter",
    )(*acts, dy, mask, lt, r, left)


def exchange(x, axis, size, bit):
    return lax.ppermute(x, axis, [(i, i ^ bit) for i in range(size)])


def per_device(act, dy, weight, code, left_factor, right_factor, *, rows, cols):
    bits = [1 << b for b in range(cols.bit_length() - 1)]
    hid, width = weight.shape
    tall, short = act.shape[0], dy.shape[0]
    tokens = tall * cols
    lt = left_factor.T

    parts = {0: act}
    for bit in reversed(bits):
        parts.update({k | bit: exchange(v, "col", cols, bit) for k, v in list(parts.items())})
    acts = [parts[k] for k in range(cols)]

    ring = list(range(0, rows, 2)) + list(range(1, rows, 2))[::-1]
    up = [(ring[i], ring[(i + 1) % rows]) for i in range(rows)]
    down = [(b, a) for a, b in up]
    blocks = {0: dy}
    for step in range(1, rows // 2 + 1):
        blocks[-step] = lax.ppermute(blocks[1 - step], "row", up)
        if step < rows - step:
            blocks[step] = lax.ppermute(blocks[step - 1], "row", down)
    me = lax.axis_index("row")
    place = jnp.where(me % 2 == 0, me // 2, rows - 1 - me // 2)
    steps = sorted(blocks)
    spot = (place + jnp.array(steps, jnp.int32)) % rows
    source = jnp.where(spot < (rows + 1) // 2, 2 * spot, 2 * (rows - 1 - spot) + 1)
    start = source * short
    at = ((start // tall) ^ lax.axis_index("col")) * tall + start % tall

    merged, mask = merge(code, weight, lt, right_factor)
    all_dy = join(at.astype(jnp.int32), [blocks[s] for s in steps])

    pieces = []
    n_back = 2
    for i in range(n_back):
        count = hid // n_back
        keep, send = back(all_dy, merged, i * count, count, tall)
        for bit in bits:
            total = keep.reshape(-1, tall, count) + exchange(send, "col", cols, bit).reshape(-1, tall, count).astype(F32)
            keep, send = total[0::2], total[1::2].astype(BF16)
        pieces.append(keep[0].astype(BF16))
    input_grad = jnp.concatenate(pieces, axis=1)

    left = jnp.zeros(lt.shape, F32)
    rights = []
    n_col = 2
    for i in range(n_col):
        count = width // n_col
        left, right = adapter(acts, all_dy, mask, lt, right_factor, left, i * count, count)
        for b in range(rows.bit_length() - 1):
            right = right + exchange(right, "row", rows, 1 << b)
        rights.append(right)
    for bit in bits:
        left = left + exchange(left, "col", cols, bit)
    return input_grad, left.T, jnp.concatenate(rights, axis=1)


def solution(mesh):
    in_specs = (
        P("col", "row"),
        P("row", "col"),
        P("row", "col"),
        P("row", "col"),
        P("row", None),
        P(None, "col"),
    )
    out_specs = (P("col", "row"), P("row", None), P(None, "col"))
    body = functools.partial(per_device, rows=mesh.shape["row"], cols=mesh.shape["col"])
    return jax.shard_map(body, mesh=mesh, in_specs=in_specs, out_specs=out_specs, check_vma=False)
```

time: 336 us -> 149 us (0.44)
  waiting for transfers between devices: 132 us -> 47.9 us
  Pallas kernels: 0 us -> 70.5 us
  local copies, waits for them, and re-layouts: 70.4 us -> 1.43 us
  other arithmetic: 62.8 us -> 4.29 us
  matrix products: 55.6 us -> 0 us
  starting transfers between devices: 0.2 us -> 22.6 us
  between operations: 13.8 us -> 0.83 us
    psum x2 -> x0, waiting for transfers between devices: 107 us -> none  [the longest x1 74.2 us: per_device(): right_grad = lax.psum(right_partial, 'row')]
    pallas_call x0 -> x6, Pallas kernels: none -> 70.5 us  [the longest x1 23.3 us: merge(): pl.pallas_call(merge_kernel, grid=(hid // th,), in_specs=[pl.BlockSpec((t...]
    dot_general x4 -> x0, matrix products: 55.6 us -> none  [the longest x1 21.5 us: input_sums_of(): lax.dot_general(grad_rows, merged, (((1,), (1,)), ((), ())), preferred_el...]
    ppermute x0 -> x22, waiting for transfers between devices: none -> 47.9 us  [the longest x15 35.2 us: exchange(): return lax.ppermute(x, axis, [(i, i ^ bit) for i in range(size)])]
    another operation x1 -> x0, local copies, waits for them, and re-layouts: 33.6 us -> none  [expand_mask(): stacked = jnp.stack(groups, axis=1)]
    reshape x1 -> x0, local copies, waits for them, and re-layouts: 33.5 us -> none  [expand_mask(): return stacked.reshape(code.shape[0] * 4, code.shape[1])]
    another operation x5 -> x0, other arithmetic: 33.3 us -> none  [expand_mask(): stacked = jnp.stack(groups, axis=1)]
    convert_element_type x2, other arithmetic: 29.4 us -> 0.15 us  [per_device(): pieces.append(keep[0].astype(BF16))]
  transfers between devices with their start and end apart: 5 -> 22, of which waited for: 3 -> 7; matrix products, arithmetic and copies ran while one was open for 44% -> 3% of each run, Pallas kernels for 0% -> 48%
where the time goes in v1:
time: 149 us; the launch traced here: 148 us
  Pallas kernels  70.5 us (47%)
  waiting for transfers between devices  47.9 us (32%)
  starting transfers between devices  22.6 us (15%)
  other arithmetic  4.29 us (3%)
    ppermute x15, waiting for transfers between devices, exchange(): return lax.ppermute(x, axis, [(i, i ^ bit) for i in range(size)])  35.2 us
    pallas_call x1, Pallas kernels, merge(): pl.pallas_call(merge_kernel, grid=(hid // th,), in_specs=[pl.BlockSpec((t...  23.3 us
    pallas_call x2, Pallas kernels, adapter(): pl.pallas_call(functools.partial(adapter_kernel, parts=len(acts), scale=1...  23.1 us
    pallas_call x2, Pallas kernels, back(): pl.pallas_call(functools.partial(back_kernel, tall=tall), grid=(count //...  19.6 us
    ppermute x15, starting transfers between devices, exchange(): return lax.ppermute(x, axis, [(i, i ^ bit) for i in range(size)])  14.9 us
    ppermute x3, waiting for transfers between devices, per_device(): blocks[step] = lax.ppermute(blocks[step - 1], 'row', down)  6.81 us
    ppermute x4, waiting for transfers between devices, per_device(): blocks[-step] = lax.ppermute(blocks[1 - step], 'row', up)  5.96 us
    pallas_call x1, Pallas kernels, join(): pl.pallas_call(join_kernel, grid_spec=pltpu.PrefetchScalarGridSpec(num_sc...  4.52 us
  transfers between devices with their start and end apart: 22, of which 7 were waited for; matrix products, arithmetic and copies ran while one was open for 3% of the time, Pallas kernels for 48%

profile of v1, /device:TPU:0, one launch (start us, length us, event | category | flops | bytes accessed | tf_op | source)
XLA Modules:
  0.0 147.5 jit_solution(9466385773233961665)
XLA Ops:
  0.6 3.0 %collective-permute-start.12 = (bf16[128,3584]{1,0:T(8,128)(2,1)}, bf16[128,3584]{1,0:T(8,128)(2,1)S(1)}, u32[]{:S(2)}, u32[]{:S(2)}) collective-permute-start(bf16[128,3584]{1,0:T(8,128)(2,1)} %refs_0_.3), channel_id=1, source_target_pairs={{0,2},{1,3},{2,0},{3,1},{4,6},{5,7},{6,4},{7,5},{8,10},{9,11},{10,... | collective-permute-start | bytes 2752520 | tf_op jit(solution)/shard_map/ppermute | solution.py:182
  3.7 1.6 %collective-permute-start = (bf16[64,2048]{1,0:T(8,128)(2,1)}, bf16[64,2048]{1,0:T(8,128)(2,1)S(1)}, u32[]{:S(2)}, u32[]{:S(2)}) collective-permute-start(bf16[64,2048]{1,0:T(8,128)(2,1)} %refs_4_.1), channel_id=1, source_target_pairs={{0,8},{8,16},{16,24},{24,28},{28,20},{20,12},{12,4},{4,0},{1,9},{9... | collective-permute-start | bytes 786440 | tf_op jit(solution)/shard_map/ppermute | solution.py:202
  5.7 5.9 %collective-permute-done.refs_3_ = bf16[64,2048]{1,0:T(8,128)(2,1)S(1)} collective-permute-done((bf16[64,2048]{1,0:T(8,128)(2,1)}, bf16[64,2048]{1,0:T(8,128)(2,1)S(1)}, u32[]{:S(2)}, u32[]{:S(2)}) %collective-permute-start) | collective-permute-done | bytes 262176 | tf_op jit(solution)/shard_map/ppermute | solution.py:202
  11.6 1.6 %collective-permute-start.1 = (bf16[64,2048]{1,0:T(8,128)(2,1)S(1)}, bf16[64,2048]{1,0:T(8,128)(2,1)S(1)}, u32[]{:S(2)}, u32[]{:S(2)}) collective-permute-start(bf16[64,2048]{1,0:T(8,128)(2,1)S(1)} %collective-permute-done.refs_3_), channel_id=1, source_target_pairs={{0,8},{8,16},{16,24},{24,28},{28,20},{20,12},{12,4},{4,0},{1,9},{9... | collective-permute-start | bytes 786440 | tf_op jit(solution)/shard_map/ppermute | solution.py:202
  13.2 11.0 %collective-permute-done.12.refs_2_ = bf16[128,3584]{1,0:T(8,128)(2,1)S(1)} collective-permute-done((bf16[128,3584]{1,0:T(8,128)(2,1)}, bf16[128,3584]{1,0:T(8,128)(2,1)S(1)}, u32[]{:S(2)}, u32[]{:S(2)}) %collective-permute-start.12) | collective-permute-done | bytes 917536 | tf_op jit(solution)/shard_map/ppermute | solution.py:182
  24.2 1.8 %collective-permute-start.5 = (bf16[64,2048]{1,0:T(8,128)(2,1)S(1)}, bf16[64,2048]{1,0:T(8,128)(2,1)}, u32[]{:S(2)}, u32[]{:S(2)}) collective-permute-start(bf16[64,2048]{1,0:T(8,128)(2,1)S(1)} %collective-permute-done.4.refs_5_), channel_id=1, source_target_pairs={{8,0},{16,8},{24,16},{28,24},{20,28},{12,20},{4,12},{0,4},{9,1},{1... | collective-permute-start | bytes 786440 | tf_op jit(solution)/shard_map/ppermute | solution.py:204
  26.3 6.8 %collective-permute-done.5.refs_6_ = bf16[64,2048]{1,0:T(8,128)(2,1)} collective-permute-done((bf16[64,2048]{1,0:T(8,128)(2,1)S(1)}, bf16[64,2048]{1,0:T(8,128)(2,1)}, u32[]{:S(2)}, u32[]{:S(2)}) %collective-permute-start.5) | collective-permute-done | bytes 262176 | tf_op jit(solution)/shard_map/ppermute | solution.py:204
  33.1 1.7 %collective-permute-start.6 = (bf16[64,2048]{1,0:T(8,128)(2,1)}, bf16[64,2048]{1,0:T(8,128)(2,1)}, u32[]{:S(2)}, u32[]{:S(2)}) collective-permute-start(bf16[64,2048]{1,0:T(8,128)(2,1)} %collective-permute-done.5.refs_6_), channel_id=1, source_target_pairs={{8,0},{16,8},{24,16},{28,24},{20,28},{12,20},{4,12},{0,4},{9,1},{1... | collective-permute-start | bytes 786440 | tf_op jit(solution)/shard_map/ppermute | solution.py:204
  35.2 23.3 %merge.1 = (bf16[3584,2048]{1,0:T(8,128)(2,1)}, bf16[3584,2048]{1,0:T(8,128)(2,1)}) custom-call(s32[896,2048]{1,0:T(8,128)} %code_ref.1, bf16[3584,2048]{1,0:T(8,128)(2,1)} %w_ref.1, bf16[16,3584]{1,0:T(8,128)(2,1)} %bitcast.27, bf16[16,2048]{1,0:T(8,128)(2,1)} %refs_7_.3), custom_call_target="tpu_custom_call" | custom-call | flops 234881024 | bytes 66060288 | tf_op jit(solution)/shard_map/merge/pallas_call | solution.py:56
  59.0 4.5 %join.1.dy_ref.refs_4_ = bf16[512,2048]{1,0:T(8,128)(2,1)} custom-call(s32[8]{0:T(128)} %fusion.8.at_ref, bf16[64,2048]{1,0:T(8,128)(2,1)} %collective-permute-done.3.refs_0_, bf16[64,2048]{1,0:T(8,128)(2,1)} %collective-permute-done.2.refs_1_, bf16[64,2048]{1,0:T(8,128)(2,1)} %copy-done.7, bf16[64,2048]{1,0:T(8,128)(2,1)} %copy-done.5, ...), custom_call_target="tpu_custom_call" | custom-call | bytes 4194304 | tf_op jit(solution)/shard_map/join/pallas_call | solution.py:85
  63.6 9.7 %back.3 = (f32[256,1792]{1,0:T(8,128)}, bf16[256,1792]{1,0:T(8,128)(2,1)}) custom-call(bf16[512,2048]{1,0:T(8,128)(2,1)} %join.1.dy_ref.refs_4_, bf16[3584,2048]{1,0:T(8,128)(2,1)} %get-tuple-element.13.m_ref), custom_call_target="tpu_custom_call" | custom-call | flops 3758096384 | bytes 7340032 | tf_op jit(solution)/shard_map/back/pallas_call | solution.py:110
  74.6 11.5 %adapter.2 = (f32[16,3584]{1,0:T(8,128)}, f32[16,1024]{1,0:T(8,128)}) custom-call(bf16[128,3584]{1,0:T(8,128)(2,1)} %refs_0_.3, bf16[128,3584]{1,0:T(8,128)(2,1)} %copy-done.1, bf16[128,3584]{1,0:T(8,128)(2,1)} %copy-done, bf16[128,3584]{1,0:T(8,128)(2,1)} %copy-done.2, bf16[512,2048]{1,0:T(8,128)(2,1)} %join.1.dy_ref.refs_4_, ...), custom_call_target="tpu_custom_call" | custom-call | flops 4227858432 | bytes 7340032 | tf_op jit(solution)/shard_map/adapter/pallas_call | solution.py:156
  86.2 11.5 %adapter.3 = (f32[16,3584]{1,0:T(8,128)}, f32[16,1024]{1,0:T(8,128)}) custom-call(bf16[128,3584]{1,0:T(8,128)(2,1)} %refs_0_.3, bf16[128,3584]{1,0:T(8,128)(2,1)} %copy-done.1, bf16[128,3584]{1,0:T(8,128)(2,1)} %copy-done, bf16[128,3584]{1,0:T(8,128)(2,1)} %copy-done.2, bf16[512,2048]{1,0:T(8,128)(2,1)} %join.1.dy_ref.refs_4_, ...), custom_call_target="tpu_custom_call" | custom-call | flops 4227858432 | bytes 7340032 | tf_op jit(solution)/shard_map/adapter/pallas_call | solution.py:156
  97.7 1.8 %collective-permute-start.19 = (f32[16,1024]{1,0:T(8,128)}, f32[16,1024]{1,0:T(8,128)S(1)}, u32[]{:S(2)}, u32[]{:S(2)}) collective-permute-start(f32[16,1024]{1,0:T(8,128)} %get-tuple-element.22), channel_id=1, source_target_pairs={{0,4},{4,0},{8,12},{12,8},{16,20},{20,16},{24,28},{28,24},{1,5},{5... | collective-permute-start | bytes 196616 | tf_op jit(solution)/shard_map/ppermute | solution.py:182
  99.8 2.9 %collective-permute-done.19 = f32[16,1024]{1,0:T(8,128)S(1)} collective-permute-done((f32[16,1024]{1,0:T(8,128)}, f32[16,1024]{1,0:T(8,128)S(1)}, u32[]{:S(2)}, u32[]{:S(2)}) %collective-permute-start.19) | collective-permute-done | bytes 65568 | tf_op jit(solution)/shard_map/ppermute | solution.py:182
  103.5 2.0 %collective-permute-start.20 = (f32[16,1024]{1,0:T(8,128)S(1)}, f32[16,1024]{1,0:T(8,128)S(1)}, u32[]{:S(2)}, u32[]{:S(2)}) collective-permute-start(f32[16,1024]{1,0:T(8,128)S(1)} %add.82), channel_id=1, source_target_pairs={{0,8},{4,12},{8,0},{12,4},{16,24},{20,28},{24,16},{28,20},{1,9},{5... | collective-permute-start | bytes 196616 | tf_op jit(solution)/shard_map/ppermute | solution.py:182
  105.7 9.9 %back.2 = (f32[256,1792]{1,0:T(8,128)}, bf16[256,1792]{1,0:T(8,128)(2,1)}) custom-call(bf16[512,2048]{1,0:T(8,128)(2,1)} %join.1.dy_ref.refs_4_, bf16[3584,2048]{1,0:T(8,128)(2,1)} %get-tuple-element.13.m_ref), custom_call_target="tpu_custom_call" | custom-call | flops 3758096384 | bytes 7340032 | tf_op jit(solution)/shard_map/back/pallas_call | solution.py:110
  116.1 3.0 %collective-permute-start.21 = (f32[16,1024]{1,0:T(8,128)S(1)}, f32[16,1024]{1,0:T(8,128)S(1)}, u32[]{:S(2)}, u32[]{:S(2)}) collective-permute-start(f32[16,1024]{1,0:T(8,128)S(1)} %add.83), channel_id=1, source_target_pairs={{0,16},{4,20},{8,24},{12,28},{16,0},{20,4},{24,8},{28,12},{1,17},{... | collective-permute-start | bytes 196616 | tf_op jit(solution)/shard_map/ppermute | solution.py:182
  119.4 1.9 %collective-permute-start.10 = (bf16[1,128,1792]{2,1,0:T(8,128)(2,1)S(1)}, bf16[1,128,1792]{2,1,0:T(8,128)(2,1)S(1)}, u32[]{:S(2)}, u32[]{:S(2)}) collective-permute-start(bf16[1,128,1792]{2,1,0:T(8,128)(2,1)S(1)} %fusion.7), channel_id=1, source_target_pairs={{0,2},{1,3},{2,0},{3,1},{4,6},{5,7},{6,4},{7,5},{8,10},{9,11},{10,... | collective-permute-start | bytes 1376264 | tf_op jit(solution)/shard_map/ppermute | solution.py:182
  121.5 1.3 collective-permute-start.15
  123.7 1.9 %collective-permute-done.18 = f32[16,1024]{1,0:T(8,128)S(1)} collective-permute-done((f32[16,1024]{1,0:T(8,128)S(1)}, f32[16,1024]{1,0:T(8,128)S(1)}, u32[]{:S(2)}, u32[]{:S(2)}) %collective-permute-start.18) | collective-permute-done | bytes 65568 | tf_op jit(solution)/shard_map/ppermute | solution.py:182
  126.3 11.5 %collective-permute-done.15 = f32[16,3584]{1,0:T(8,128)S(1)} collective-permute-done((f32[16,3584]{1,0:T(8,128)S(1)}, f32[16,3584]{1,0:T(8,128)S(1)}, u32[]{:S(2)}, u32[]{:S(2)}) %collective-permute-start.15) | collective-permute-done | bytes 229408 | tf_op jit(solution)/shard_map/ppermute | solution.py:182
  138.6 7.9 %collective-permute-done.8 = bf16[1,128,1792]{2,1,0:T(8,128)(2,1)S(1)} collective-permute-done((bf16[1,128,1792]{2,1,0:T(8,128)(2,1)S(1)}, bf16[1,128,1792]{2,1,0:T(8,128)(2,1)S(1)}, u32[]{:S(2)}, u32[]{:S(2)}) %collective-permute-start.8) | collective-permute-done | bytes 458784 | tf_op jit(solution)/shard_map/ppermute | solution.py:182
  146.5 1.0 pad_maximum_fusion
  (66 shorter events, 7.8 us)
Async XLA Ops:
  0.6 23.6 %collective-permute-start.12 = (bf16[128,3584]{1,0:T(8,128)(2,1)}, bf16[128,3584]{1,0:T(8,128)(2,1)S(1)}, u32[]{:S(2)}, u32[]{:S(2)}) collective-permute-start(bf16[128,3584]{1,0:T(8,128)(2,1)} %refs_0_.3), channel_id=1, source_target_pairs={{0,2},{1,3},{2,0},{3,1},{4,6},{5,7},{6,4},{7,5},{8,10},{9,11},{10,... | collective-permute-start | bytes 2752520 | tf_op jit(solution)/shard_map/ppermute | solution.py:182
  3.7 8.0 %collective-permute-start = (bf16[64,2048]{1,0:T(8,128)(2,1)}, bf16[64,2048]{1,0:T(8,128)(2,1)S(1)}, u32[]{:S(2)}, u32[]{:S(2)}) collective-permute-start(bf16[64,2048]{1,0:T(8,128)(2,1)} %refs_4_.1), channel_id=1, source_target_pairs={{0,8},{8,16},{16,24},{24,28},{28,20},{20,12},{12,4},{4,0},{1,9},{9... | collective-permute-start | bytes 786440 | tf_op jit(solution)/shard_map/ppermute | solution.py:202
  5.2 19.0 %collective-permute-start.4 = (bf16[64,2048]{1,0:T(8,128)(2,1)}, bf16[64,2048]{1,0:T(8,128)(2,1)S(1)}, u32[]{:S(2)}, u32[]{:S(2)}) collective-permute-start(bf16[64,2048]{1,0:T(8,128)(2,1)} %refs_4_.1), channel_id=1, source_target_pairs={{8,0},{16,8},{24,16},{28,24},{20,28},{12,20},{4,12},{0,4},{9,1},{1... | collective-permute-start | bytes 786440 | tf_op jit(solution)/shard_map/ppermute | solution.py:204
  11.6 46.8 %copy-start.5 = (bf16[64,2048]{1,0:T(8,128)(2,1)}, bf16[64,2048]{1,0:T(8,128)(2,1)S(1)}, u32[]{:S(2)}) copy-start(bf16[64,2048]{1,0:T(8,128)(2,1)S(1)} %collective-permute-done.refs_3_) | copy-start | bytes 786436
  11.6 14.4 %collective-permute-start.1 = (bf16[64,2048]{1,0:T(8,128)(2,1)S(1)}, bf16[64,2048]{1,0:T(8,128)(2,1)S(1)}, u32[]{:S(2)}, u32[]{:S(2)}) collective-permute-start(bf16[64,2048]{1,0:T(8,128)(2,1)S(1)} %collective-permute-done.refs_3_), channel_id=1, source_target_pairs={{0,8},{8,16},{16,24},{24,28},{28,20},{20,12},{12,4},{4,0},{1,9},{9... | collective-permute-start | bytes 786440 | tf_op jit(solution)/shard_map/ppermute | solution.py:202
  13.2 60.1 %collective-permute-start.11 = (bf16[128,3584]{1,0:T(8,128)(2,1)}, bf16[128,3584]{1,0:T(8,128)(2,1)S(1)}, u32[]{:S(2)}, u32[]{:S(2)}) collective-permute-start(bf16[128,3584]{1,0:T(8,128)(2,1)} %refs_0_.3), channel_id=1, source_target_pairs={{0,1},{1,0},{2,3},{3,2},{4,5},{5,4},{6,7},{7,6},{8,9},{9,8},{10,11... | collective-permute-start | bytes 2752520 | tf_op jit(solution)/shard_map/ppermute | solution.py:182
  24.2 34.2 %copy-start = (bf16[128,3584]{1,0:T(8,128)(2,1)}, bf16[128,3584]{1,0:T(8,128)(2,1)S(1)}, u32[]{:S(2)}) copy-start(bf16[128,3584]{1,0:T(8,128)(2,1)S(1)} %collective-permute-done.12.refs_2_) | copy-start | bytes 2752516
  24.2 49.1 %collective-permute-start.13 = (bf16[128,3584]{1,0:T(8,128)(2,1)S(1)}, bf16[128,3584]{1,0:T(8,128)(2,1)S(1)}, u32[]{:S(2)}, u32[]{:S(2)}) collective-permute-start(bf16[128,3584]{1,0:T(8,128)(2,1)S(1)} %collective-permute-done.12.refs_2_), channel_id=1, source_target_pairs={{0,1},{1,0},{2,3},{3,2},{4,5},{5,4},{6,7},{7,6},{8,9},{9,8},{10,11... | collective-permute-start | bytes 2752520 | tf_op jit(solution)/shard_map/ppermute | solution.py:182
  24.2 8.9 %collective-permute-start.5 = (bf16[64,2048]{1,0:T(8,128)(2,1)S(1)}, bf16[64,2048]{1,0:T(8,128)(2,1)}, u32[]{:S(2)}, u32[]{:S(2)}) collective-permute-start(bf16[64,2048]{1,0:T(8,128)(2,1)S(1)} %collective-permute-done.4.refs_5_), channel_id=1, source_target_pairs={{8,0},{16,8},{24,16},{28,24},{20,28},{12,20},{4,12},{0,4},{9,1},{1... | collective-permute-start | bytes 786440 | tf_op jit(solution)/shard_map/ppermute | solution.py:204
  26.1 8.8 %collective-permute-start.2 = (bf16[64,2048]{1,0:T(8,128)(2,1)S(1)}, bf16[64,2048]{1,0:T(8,128)(2,1)}, u32[]{:S(2)}, u32[]{:S(2)}) collective-permute-start(bf16[64,2048]{1,0:T(8,128)(2,1)S(1)} %collective-permute-done.1.refs_2_), channel_id=1, source_target_pairs={{0,8},{8,16},{16,24},{24,28},{28,20},{20,12},{12,4},{4,0},{1,9},{9... | collective-permute-start | bytes 786440 | tf_op jit(solution)/shard_map/ppermute | solution.py:202
  33.1 25.9 %collective-permute-start.6 = (bf16[64,2048]{1,0:T(8,128)(2,1)}, bf16[64,2048]{1,0:T(8,128)(2,1)}, u32[]{:S(2)}, u32[]{:S(2)}) collective-permute-start(bf16[64,2048]{1,0:T(8,128)(2,1)} %collective-permute-done.5.refs_6_), channel_id=1, source_target_pairs={{8,0},{16,8},{24,16},{28,24},{20,28},{12,20},{4,12},{0,4},{9,1},{1... | collective-permute-start | bytes 786440 | tf_op jit(solution)/shard_map/ppermute | solution.py:204
  34.8 24.2 %collective-permute-start.3 = (bf16[64,2048]{1,0:T(8,128)(2,1)}, bf16[64,2048]{1,0:T(8,128)(2,1)}, u32[]{:S(2)}, u32[]{:S(2)}) collective-permute-start(bf16[64,2048]{1,0:T(8,128)(2,1)} %collective-permute-done.2.refs_1_), channel_id=1, source_target_pairs={{0,8},{8,16},{16,24},{24,28},{28,20},{20,12},{12,4},{4,0},{1,9},{9... | collective-permute-start | bytes 786440 | tf_op jit(solution)/shard_map/ppermute | solution.py:202
  73.3 45.9 %collective-permute-start.9 = (bf16[256,1792]{1,0:T(8,128)(2,1)}, bf16[256,1792]{1,0:T(8,128)(2,1)S(1)}, u32[]{:S(2)}, u32[]{:S(2)}) collective-permute-start(bf16[256,1792]{1,0:T(8,128)(2,1)} %get-tuple-element.17), channel_id=1, source_target_pairs={{0,1},{1,0},{2,3},{3,2},{4,5},{5,4},{6,7},{7,6},{8,9},{9,8},{10,11... | collective-permute-start | bytes 2752520 | tf_op jit(solution)/shard_map/ppermute | solution.py:182
  97.7 5.0 %collective-permute-start.19 = (f32[16,1024]{1,0:T(8,128)}, f32[16,1024]{1,0:T(8,128)S(1)}, u32[]{:S(2)}, u32[]{:S(2)}) collective-permute-start(f32[16,1024]{1,0:T(8,128)} %get-tuple-element.22), channel_id=1, source_target_pairs={{0,4},{4,0},{8,12},{12,8},{16,20},{20,16},{24,28},{28,24},{1,5},{5... | collective-permute-start | bytes 196616 | tf_op jit(solution)/shard_map/ppermute | solution.py:182
  99.5 6.0 %collective-permute-start.16 = (f32[16,1024]{1,0:T(8,128)S(1)}, f32[16,1024]{1,0:T(8,128)S(1)}, u32[]{:S(2)}, u32[]{:S(2)}) collective-permute-start(f32[16,1024]{1,0:T(8,128)S(1)} %copy-done.9), channel_id=1, source_target_pairs={{0,4},{4,0},{8,12},{12,8},{16,20},{20,16},{24,28},{28,24},{1,5},{5... | collective-permute-start | bytes 196616 | tf_op jit(solution)/shard_map/ppermute | solution.py:182
  103.5 12.6 %collective-permute-start.20 = (f32[16,1024]{1,0:T(8,128)S(1)}, f32[16,1024]{1,0:T(8,128)S(1)}, u32[]{:S(2)}, u32[]{:S(2)}) collective-permute-start(f32[16,1024]{1,0:T(8,128)S(1)} %add.82), channel_id=1, source_target_pairs={{0,8},{4,12},{8,0},{12,4},{16,24},{20,28},{24,16},{28,20},{1,9},{5... | collective-permute-start | bytes 196616 | tf_op jit(solution)/shard_map/ppermute | solution.py:182
  105.5 13.6 %collective-permute-start.17 = (f32[16,1024]{1,0:T(8,128)S(1)}, f32[16,1024]{1,0:T(8,128)S(1)}, u32[]{:S(2)}, u32[]{:S(2)}) collective-permute-start(f32[16,1024]{1,0:T(8,128)S(1)} %add.79), channel_id=1, source_target_pairs={{0,8},{4,12},{8,0},{12,4},{16,24},{20,28},{24,16},{28,20},{1,9},{5... | collective-permute-start | bytes 196616 | tf_op jit(solution)/shard_map/ppermute | solution.py:182
  115.6 5.7 %collective-permute-start.7 = (bf16[256,1792]{1,0:T(8,128)(2,1)}, bf16[256,1792]{1,0:T(8,128)(2,1)S(1)}, u32[]{:S(2)}, u32[]{:S(2)}) collective-permute-start(bf16[256,1792]{1,0:T(8,128)(2,1)} %get-tuple-element.15), channel_id=1, source_target_pairs={{0,1},{1,0},{2,3},{3,2},{4,5},{5,4},{6,7},{7,6},{8,9},{9,8},{10,11... | collective-permute-start | bytes 2752520 | tf_op jit(solution)/shard_map/ppermute | solution.py:182
  115.6 5.9 %collective-permute-start.14 = (f32[16,3584]{1,0:T(8,128)S(1)}, f32[16,3584]{1,0:T(8,128)S(1)}, u32[]{:S(2)}, u32[]{:S(2)}) collective-permute-start(f32[16,3584]{1,0:T(8,128)S(1)} %copy-done.8), channel_id=1, source_target_pairs={{0,1},{1,0},{2,3},{3,2},{4,5},{5,4},{6,7},{7,6},{8,9},{9,8},{10,11... | collective-permute-start | bytes 688136 | tf_op jit(solution)/shard_map/ppermute | solution.py:182
  116.1 7.6 %collective-permute-start.21 = (f32[16,1024]{1,0:T(8,128)S(1)}, f32[16,1024]{1,0:T(8,128)S(1)}, u32[]{:S(2)}, u32[]{:S(2)}) collective-permute-start(f32[16,1024]{1,0:T(8,128)S(1)} %add.83), channel_id=1, source_target_pairs={{0,16},{4,20},{8,24},{12,28},{16,0},{20,4},{24,8},{28,12},{1,17},{... | collective-permute-start | bytes 196616 | tf_op jit(solution)/shard_map/ppermute | solution.py:182
  119.1 6.5 %collective-permute-start.18 = (f32[16,1024]{1,0:T(8,128)S(1)}, f32[16,1024]{1,0:T(8,128)S(1)}, u32[]{:S(2)}, u32[]{:S(2)}) collective-permute-start(f32[16,1024]{1,0:T(8,128)S(1)} %add.80), channel_id=1, source_target_pairs={{0,16},{4,20},{8,24},{12,28},{16,0},{20,4},{24,8},{28,12},{1,17},{... | collective-permute-start | bytes 196616 | tf_op jit(solution)/shard_map/ppermute | solution.py:182
  119.4 19.1 %collective-permute-start.10 = (bf16[1,128,1792]{2,1,0:T(8,128)(2,1)S(1)}, bf16[1,128,1792]{2,1,0:T(8,128)(2,1)S(1)}, u32[]{:S(2)}, u32[]{:S(2)}) collective-permute-start(bf16[1,128,1792]{2,1,0:T(8,128)(2,1)S(1)} %fusion.7), channel_id=1, source_target_pairs={{0,2},{1,3},{2,0},{3,1},{4,6},{5,7},{6,4},{7,5},{8,10},{9,11},{10,... | collective-permute-start | bytes 1376264 | tf_op jit(solution)/shard_map/ppermute | solution.py:182
  121.5 16.3 %collective-permute-start.15 = (f32[16,3584]{1,0:T(8,128)S(1)}, f32[16,3584]{1,0:T(8,128)S(1)}, u32[]{:S(2)}, u32[]{:S(2)}) collective-permute-start(f32[16,3584]{1,0:T(8,128)S(1)} %add.77), channel_id=1, source_target_pairs={{0,2},{1,3},{2,0},{3,1},{4,6},{5,7},{6,4},{7,5},{8,10},{9,11},{10,... | collective-permute-start | bytes 688136 | tf_op jit(solution)/shard_map/ppermute | solution.py:182
  122.8 23.6 %collective-permute-start.8 = (bf16[1,128,1792]{2,1,0:T(8,128)(2,1)S(1)}, bf16[1,128,1792]{2,1,0:T(8,128)(2,1)S(1)}, u32[]{:S(2)}, u32[]{:S(2)}) collective-permute-start(bf16[1,128,1792]{2,1,0:T(8,128)(2,1)S(1)} %fusion.5), channel_id=1, source_target_pairs={{0,2},{1,3},{2,0},{3,1},{4,6},{5,7},{6,4},{7,5},{8,10},{9,11},{10,... | collective-permute-start | bytes 1376264 | tf_op jit(solution)/shard_map/ppermute | solution.py:182
  (9 other events, 131.5 us)
